TPU v7x, 32 devices: a whole 2x2x4 slice. The times are simulated.
32 devices in a mesh: rows: 2 (over y), cols: 16 (over z, x, core).
Axes of the slice: x: 2, y: 2, z: 4, core: 2. Of those that a mesh axis runs over, the one named last changes fastest.
Arguments:
- eigvecs: float32 [1024, 2048], P('rows', 'cols'), may hold values from -6 to 6
- wy_packed: float32 [32, 128, 128], P(('rows', 'cols')), may hold values from -6 to 6
- slot_block: int32 [2, 8, 2], P('rows'), may hold values from 0 to 1, each once within a row
Outputs:
- transformed: float32 [1024, 2048], P('rows', 'cols')
Inputs may be any that keep to these rules, and one draw needn't show every extreme that they name: `slot_block`: for every group and level the 2 entries name each of 0 .. 1 once.
All inputs are finite; a program needn't handle non-finite values.
Results may differ from a plain program's by a relative error of at most 0.0003.
Values sent between devices are 32-bit elements; how exact they have to be, the bound alone decides.
A program may use at most 64 MiB of HBM per device.

v0:
```python
import functools

import jax
import jax.numpy as jnp
from jax import lax
from jax.experimental import pallas as pl
from jax.experimental.pallas import tpu as pltpu
from jax.sharding import PartitionSpec as P

MESH = pl.DeviceIdType.MESH
F32 = jnp.float32
BF16 = jnp.bfloat16
NN = (((1,), (0,)), ((), ()))
NT = (((1,), (1,)), ((), ()))


def split(value):
    high = value.astype(BF16)
    low = (value - high.astype(F32)).astype(BF16)
    return high, low


def product(a, b, dims=NN):
    dot = functools.partial(lax.dot_general, dimension_numbers=dims, preferred_element_type=F32)
    if dims == NN:
        stacked = jnp.concatenate([a[0], a[1]], axis=1)
        return dot(stacked, jnp.concatenate([b[0], b[0]], axis=0)) + dot(a[0], b[1])
    return dot(a[0], b[0]) + (dot(a[0], b[1]) + dot(a[1], b[0]))


def inverses(grams, multiply):
    band = grams[0].shape[0]
    row = lax.broadcasted_iota(jnp.int32, (band, band), 0)
    col = lax.broadcasted_iota(jnp.int32, (band, band), 1)
    zero = jnp.zeros((band, band), F32)
    diagonal = row == col
    stricts, found = [], []
    for gram in grams:
        on_diagonal = jnp.where(diagonal, 0.5 * gram, zero)
        by_row = 1.0 / jnp.sum(on_diagonal, axis=1, keepdims=True)
        by_col = 1.0 / jnp.sum(on_diagonal, axis=0, keepdims=True)
        strict = jnp.where(col > row, gram, zero)
        pairs = jnp.where(row // 2 == col // 2, strict, zero)
        stricts.append(strict)
        found.append(jnp.where(diagonal, by_row, zero) - pairs * by_row * by_col)
    width = 2
    while width < band:
        factor = 4 if width * 4 <= band else 2
        wide = width * factor
        inside = (row // wide == col // wide) & (row // width != col // width)
        corners = [jnp.where(inside, strict, zero) for strict in stricts]
        powers = [multiply(a, b) for a, b in zip(found, corners)]
        firsts = [multiply(n, a) for n, a in zip(powers, found)]
        found = [a - b for a, b in zip(found, firsts)]
        if factor == 4:
            squares = [multiply(n, n) for n in powers]
            seconds = [multiply(n, a) for n, a in zip(squares, found)]
            found = [a + b for a, b in zip(found, seconds)]
        width = wide
    return found


def fast(a, b):
    return product(split(a), split(b))


def kernel(
    levels, n_rows, n_z, slot_ref, eig_ref, wy_ref, out_ref,
    wg, xt, ops, half_send, above, up_send, up_recv, down_send, down_recv,
    recv_sem, send_sem, own_sem, up_sem, down_sem, half_sem, side_sem,
):
    band = wy_ref.shape[1]
    chunks = eig_ref.shape[0] // band
    per_level = chunks // 2
    rounds = levels // 2
    g = lax.axis_index("rows")
    c = lax.axis_index("cols")
    z, x, k = c // 4, (c // 2) % 2, c % 2
    x_partner = z * 4 + (1 - x) * 2 + k
    core_partner = z * 4 + x * 2 + (1 - k)
    z_mates = [((z + d) % n_z) * 4 + x * 2 + k for d in range(1, n_z)]
    has_above = g > 0
    has_below = g < n_rows - 1

    barrier = pltpu.get_barrier_semaphore()
    for other in z_mates + [x_partner, core_partner]:
        pl.semaphore_signal(barrier, inc=1, device_id={"cols": other}, device_id_type=MESH)

    @pl.when(has_above)
    def _():
        pl.semaphore_signal(barrier, inc=1, device_id={"rows": g - 1}, device_id_type=MESH)

    @pl.when(has_below)
    def _():
        pl.semaphore_signal(barrier, inc=1, device_id={"rows": g + 1}, device_id_type=MESH)

    def block_copy(block, target, sem):
        return pltpu.make_async_remote_copy(
            src_ref=wg.at[block],
            dst_ref=wg.at[block],
            send_sem=sem,
            recv_sem=recv_sem.at[block],
            device_id={"cols": target},
            device_id_type=MESH,
        )

    def to_x(zz, xx):
        return block_copy(zz * 4 + xx * 2 + k, x_partner, send_sem.at[zz * 2 + xx, 0])

    def to_core(zz, xx):
        return block_copy(zz * 4 + xx * 2 + k, core_partner, send_sem.at[zz * 2 + xx, 1])

    def to_z(zz):
        return block_copy(c, zz * 4 + x * 2 + k, own_sem.at[zz])

    def relay_z(zz):
        @pl.when(z != zz)
        def _():
            to_x(zz, x).wait_recv()
            to_x(zz, x).start()
            to_core(zz, x).start()

    def relay_x(zz):
        to_core(zz, 1 - x).wait_recv()
        to_core(zz, 1 - x).start()

    def wait_core(zz):
        for xx in range(2):
            block_copy(zz * 4 + xx * 2 + 1 - k, core_partner, send_sem.at[0, 0]).wait_recv()

    def row_copy(src, dst, sem, at, target):
        return pltpu.make_async_remote_copy(
            src_ref=src.at[at],
            dst_ref=dst.at[at],
            send_sem=sem.at[0, at],
            recv_sem=sem.at[1, at],
            device_id={"rows": target},
            device_id_type=MESH,
        )

    def go_up(at):
        return row_copy(up_send, up_recv, up_sem, at, g - 1)

    def go_down(at):
        return row_copy(down_send, down_recv, down_sem, at, g + 1)

    half = band // 2

    def half_down(at):
        return pltpu.make_async_remote_copy(
            src_ref=half_send.at[at],
            dst_ref=above.at[at, pl.ds(k * half, half)],
            send_sem=half_sem.at[0, at],
            recv_sem=half_sem.at[1, at],
            device_id={"rows": g + 1},
            device_id_type=MESH,
        )

    def half_side(at):
        return pltpu.make_async_remote_copy(
            src_ref=above.at[at, pl.ds(k * half, half)],
            dst_ref=above.at[at, pl.ds(k * half, half)],
            send_sem=side_sem.at[0, at],
            recv_sem=side_sem.at[1, at],
            device_id={"cols": core_partner},
            device_id_type=MESH,
        )

    def send_half(at):
        level = 2 * at + 1
        first = slot_ref[0, per_level - 1, level] == 0
        rows = pl.ds(k * half, half)
        half_send[at] = jnp.where(
            first, wg[level * per_level, rows], wg[level * per_level + 1, rows]
        )
        half_down(at).start()

    wg[c] = pltpu.roll(jnp.transpose(wy_ref[0]), 0, 1, stride=1, stride_axis=0)
    pl.semaphore_wait(
        barrier, n_z + 1 + has_above.astype(jnp.int32) + has_below.astype(jnp.int32)
    )
    to_x(z, x).start()
    to_core(z, x).start()
    for far in range(n_z - 1, -1, -1):
        @pl.when((far != z) & ((far < z) | (z < 2)))
        def _():
            to_z(far).start()

    @pl.when(jnp.logical_not(has_above))
    def _():
        above[...] = jnp.zeros_like(above)
        down_recv[...] = jnp.zeros_like(down_recv)

    @pl.when(jnp.logical_not(has_below))
    def _():
        up_recv[...] = jnp.zeros_like(up_recv)

    for i in range(chunks):
        xt[i] = jnp.transpose(eig_ref[i * band : (i + 1) * band, :])

    row = lax.broadcasted_iota(jnp.int32, (band, band), 0)
    col = lax.broadcasted_iota(jnp.int32, (band, band), 1)
    upper = col >= row
    zero = jnp.zeros((band, band), F32)

    def spread(w):
        return jnp.concatenate([jnp.where(upper, w, zero), jnp.where(upper, zero, w)], axis=1)

    def chosen(level, h):
        first = slot_ref[0, h, level] == 0
        return jnp.where(first, wg[level * per_level], wg[level * per_level + 1])

    def prepare(sheared, places):
        v_parts = [split(spread(w)) for w in sheared]
        grams = [product(v, v, NT) for v in v_parts]
        factors = inverses(grams, fast)
        for place, v, t in zip(places, v_parts, factors):
            z_parts = split(product(split(t), v))
            ops[place, 0] = z_parts[0]
            ops[place, 1] = z_parts[1]
            ops[place, 2] = v[0]
            ops[place, 3] = v[1]

    def reflected(places, pairs):
        halves = [split(pair) for pair in pairs]
        projected = [
            split(product(x, (ops[p, 0], ops[p, 1]), NT)) for p, x in zip(places, halves)
        ]
        return [
            pair - product(y, (ops[p, 2], ops[p, 3]))
            for p, y, pair in zip(places, projected, pairs)
        ]

    def window(top, bottom):
        return jnp.concatenate([top, bottom], axis=1)

    relay_z(0)

    @pl.when(z >= 2)
    def _():
        for far in range(n_z - 1, 2, -1):
            @pl.when(far > z)
            def _():
                to_z(far).start()

    relay_x(0)
    wait_core(0)

    @pl.when(has_below)
    def _():
        send_half(0)

    relay_z(1)
    prepare([chosen(0, 0), chosen(0, 1)], [3, 4])

    def both_levels(at, carry):
        @pl.when(has_above)
        def _():
            half_down(at).wait_recv()
            half_side(at).start()

        upper_new, lower_new = reflected([3, 4], [window(xt[0], xt[1]), window(xt[2], xt[3])])
        xt[0], xt[1] = upper_new[:, :band], upper_new[:, band:]
        xt[2], xt[3] = lower_new[:, :band], lower_new[:, band:]

        @pl.when(has_above)
        def _():
            up_send[at] = xt[0]
            go_up(at).start()

        @pl.when(has_below)
        def _():
            down_send[at] = xt[chunks - 1]
            go_down(at).start()

        @pl.when(at < rounds - 1)
        def _():
            relay_x(at + 1)
            wait_core(at + 1)

            @pl.when(has_below)
            def _():
                send_half(at + 1)

        @pl.when(at < rounds - 2)
        def _():
            relay_z(at + 2)

        @pl.when(has_above)
        def _():
            half_side(at).wait_recv()

        odd, even = 2 * at + 1, (2 * at + 2) % levels
        prepare(
            [chosen(odd, 0), chosen(odd, 1), above[at], chosen(even, 0), chosen(even, 1)],
            [0, 1, 2, 3, 4],
        )

        @pl.when(has_below)
        def _():
            go_up(at).wait_recv()

        @pl.when(has_above)
        def _():
            go_down(at).wait_recv()

        middle, last, first = reflected(
            [0, 1, 2],
            [
                window(xt[1], xt[2]),
                window(xt[chunks - 1], up_recv[at]),
                window(down_recv[at], xt[0]),
            ],
        )
        xt[1], xt[2] = middle[:, :band], middle[:, band:]
        xt[chunks - 1] = last[:, :band]
        xt[0] = jnp.where(has_above, first[:, band:], xt[0])
        return carry

    lax.fori_loop(0, rounds, both_levels, 0)

    for i in range(chunks):
        out_ref[i * band : (i + 1) * band, :] = jnp.transpose(xt[i])

    for zz in range(n_z):
        @pl.when(z != zz)
        def _():
            to_z(zz).wait_send()

    for zz in range(n_z):
        to_x(zz, x).wait_send()
        for xx in range(2):
            to_core(zz, xx).wait_send()
    for at in range(rounds):
        @pl.when(has_above)
        def _():
            go_up(at).wait_send()
            half_side(at).wait_send()

        @pl.when(has_below)
        def _():
            go_down(at).wait_send()
            half_down(at).wait_send()


def per_device(n_rows, n_cols, eigvecs, wy_packed, slot_block):
    band = wy_packed.shape[1]
    rows, cols = eigvecs.shape
    levels, per_level = slot_block.shape[1:]
    n_z = n_cols // 4
    rounds = levels // 2
    assert n_cols == levels * per_level and n_z == rounds
    assert wy_packed.shape[0] == 1 and per_level == 2 and rows == 4 * band
    blocks = pltpu.VMEM((rounds, band, band), F32)
    slots = pltpu.VMEM((rounds, cols, band), F32)
    vmem = pl.BlockSpec(memory_space=pltpu.VMEM)
    in_order = pltpu.SemaphoreType.DMA((2, rounds))
    return pl.pallas_call(
        functools.partial(kernel, levels, n_rows, n_z),
        out_shape=jax.ShapeDtypeStruct(eigvecs.shape, F32),
        in_specs=[pl.BlockSpec(memory_space=pltpu.SMEM), vmem, vmem],
        out_specs=vmem,
        scratch_shapes=[
            pltpu.VMEM((n_cols, band, band), F32),
            pltpu.VMEM((rows // band, cols, band), F32),
            pltpu.VMEM((5, 4, band, 2 * band), BF16),
            pltpu.VMEM((rounds, band // 2, band), F32),
            blocks,
            slots,
            slots,
            slots,
            slots,
            pltpu.SemaphoreType.DMA((n_cols,)),
            pltpu.SemaphoreType.DMA((n_cols // 2, 2)),
            pltpu.SemaphoreType.DMA((n_z,)),
            in_order,
            in_order,
            in_order,
            in_order,
        ],
        compiler_params=pltpu.CompilerParams(collective_id=0, has_side_effects=True),
    )(jnp.swapaxes(slot_block, 1, 2), eigvecs, wy_packed)


def solution(mesh):
    placed = (P("rows", "cols"), P(("rows", "cols"), None, None), P("rows", None, None))
    return jax.shard_map(
        functools.partial(per_device, mesh.shape["rows"], mesh.shape["cols"]),
        mesh=mesh, in_specs=placed, out_specs=P("rows", "cols"), check_vma=False,
    )
```

profile of v0, /device:TPU:8, one launch (start us, length us, event | category | flops | bytes accessed | tf_op | source)
XLA Modules:
  0.0 38.1 jit_solution(5205965881010329202)
XLA Ops:
  0.0 36.5 %shard_map.37 = f32[512,128]{1,0:T(8,128)} custom-call(s32[1,2,8]{2,1,0:T(2,128)} %bitcast.1, f32[512,128]{1,0:T(8,128)} %eig_ref.1, f32[1,128,128]{2,1,0:T(8,128)} %wy_ref.1), custom_call_target="tpu_custom_call" | custom-call | tf_op jit(solution)/shard_map/pallas_call | solution.py:358
  36.5 1.7 %copy.5 = f32[512,128]{1,0:T(8,128)} copy(f32[512,128]{1,0:T(8,128)} %shard_map.37) | data formatting | bytes 524288
where the time goes:
time: 38.3 us; the launch traced here: 38.1 us
  Pallas kernels  36.5 us (95%)
  local copies, waits for them, and re-layouts  1.67 us (4%)
    pallas_call x1, Pallas kernels, per_device(): pl.pallas_call(functools.partial(kernel, levels, n_rows, n_z), out_shape=...  36.5 us
    unnamed x1, local copies, waits for them, and re-layouts  1.67 us

commit v1 on v0

--- a/solution.py
+++ b/solution.py
@@ -64,6 +64,235 @@
     return product(split(a), split(b))
 
 
+def spread(w):
+    band = w.shape[0]
+    row = lax.broadcasted_iota(jnp.int32, (band, band), 0)
+    col = lax.broadcasted_iota(jnp.int32, (band, band), 1)
+    upper = col >= row
+    zero = jnp.zeros((band, band), F32)
+    return jnp.concatenate([jnp.where(upper, w, zero), jnp.where(upper, zero, w)], axis=1)
+
+
+def own_blocks(sheared):
+    v_parts = [split(spread(w)) for w in sheared]
+    grams = [product(v, v, NT) for v in v_parts]
+    factors = inverses(grams, fast)
+    return [product(split(t), v) for t, v in zip(factors, v_parts)]
+
+
+def paired_kernel(
+    levels, n_z, slot_ref, eig_ref, wy_ref, out_ref,
+    raw, vz, xin, xt, ops, flags,
+    raw_recv, own_send, relay_send, core_recv, core_send, side_sem, local_sem,
+):
+    band = wy_ref.shape[1]
+    chunks = eig_ref.shape[0] // band
+    per_level = chunks // 2
+    windows = 2 * per_level
+    g = lax.axis_index("rows")
+    c = lax.axis_index("cols")
+    z, x, k = c // 4, (c // 2) % 2, c % 2
+    flip_g, flip_x = 1 - 2 * g, 1 - 2 * x
+    p1 = {"rows": g + (1 - k) * flip_g, "cols": c + k * 2 * flip_x}
+    p2 = {"rows": g + k * flip_g, "cols": c + (1 - k) * 2 * flip_x}
+    core_partner = {"rows": g, "cols": c + 1 - 2 * k}
+    row_partner = {"rows": 1 - g, "cols": c}
+
+    def z_mate(zz):
+        return {"rows": g, "cols": c + 4 * (zz - z)}
+
+    own = g * levels + z * 2 + x
+
+    local_v = pltpu.make_async_copy(wy_ref.at[0], raw.at[own], local_sem.at[0])
+    local_x = pltpu.make_async_copy(eig_ref, xin.at[g], local_sem.at[1])
+    local_v.start()
+    local_x.start()
+
+    barrier = pltpu.get_barrier_semaphore()
+    for d in range(1, n_z):
+        pl.semaphore_signal(
+            barrier, inc=1, device_id=z_mate((z + d) % n_z), device_id_type=MESH
+        )
+    for other in (p1, p2, core_partner):
+        pl.semaphore_signal(barrier, inc=1, device_id=other, device_id_type=MESH)
+
+    level_row = lax.broadcasted_iota(jnp.int32, (levels, band), 0)
+    tile = jnp.zeros((levels, band), F32)
+    for level in range(levels):
+        tile = jnp.where(level_row == level, slot_ref[0, 0, level].astype(F32), tile)
+    flags[g] = tile
+    xt[2 * chunks] = jnp.zeros((eig_ref.shape[1], band), F32)
+
+    def remote(src, dst, send, recv, target):
+        return pltpu.make_async_remote_copy(
+            src_ref=src, dst_ref=dst, send_sem=send, recv_sem=recv,
+            device_id=target, device_id_type=MESH,
+        )
+
+    def from_own(at, target):
+        return remote(wy_ref.at[0], raw.at[own], own_send.at[at], raw_recv.at[own], target)
+
+    def to_z(zz):
+        return from_own(zz, z_mate(zz))
+
+    def relay(q, zz, way, target):
+        return remote(raw.at[q], raw.at[q], relay_send.at[zz, way], raw_recv.at[q], target)
+
+    def across(q):
+        return remote(vz.at[k, q], vz.at[k, q], core_send.at[q], core_recv.at[q], core_partner)
+
+    def flags_across():
+        return remote(flags.at[g], flags.at[g], side_sem.at[0, 0], side_sem.at[1, 0], row_partner)
+
+    def x_across():
+        return remote(eig_ref, xin.at[g], side_sem.at[0, 1], side_sem.at[1, 1], row_partner)
+
+    pl.semaphore_wait(barrier, n_z + 2)
+    for zz in range(n_z - 1, -1, -1):
+        @pl.when(zz != z)
+        def _():
+            to_z(zz).start()
+    from_own(n_z, p1).start()
+    from_own(n_z + 1, p2).start()
+    flags_across().start()
+    x_across().start()
+    local_v.wait()
+
+    def line(j, carry):
+        f1, f2 = j % 2, j // 2
+        line_g = g + flip_g * (k * f2 + (1 - k) * f1)
+        line_x = x + flip_x * (k * f1 + (1 - k) * f2)
+        blocks = [line_g * levels + zz * 2 + line_x for zz in range(n_z)]
+        for zz in range(n_z - 1, -1, -1):
+            q = blocks[zz]
+
+            @pl.when((j > 0) | (zz != z))
+            def _():
+                relay(q, zz, 0, p1).wait_recv()
+
+            @pl.when((j == 0) & (zz != z))
+            def _():
+                relay(q, zz, 0, p1).start()
+                relay(q, zz, 1, p2).start()
+
+            @pl.when(j == 1)
+            def _():
+                relay(q, zz, 2, p2).start()
+
+        sheared = [pltpu.roll(jnp.transpose(raw[q]), 0, 1, stride=1, stride_axis=0) for q in blocks]
+        for q, w, zed in zip(blocks, sheared, own_blocks(sheared)):
+            vz[k, q, 0] = w
+            vz[k, q, 1] = zed[:, :band]
+            vz[k, q, 2] = zed[:, band:]
+        for q in blocks:
+            across(q).start()
+        return carry
+
+    lax.fori_loop(0, 4, line, 0)
+
+    local_x.wait()
+    x_across().wait_recv()
+    flags_across().wait_recv()
+    for r in range(2):
+        for i in range(chunks):
+            xt[r * chunks + i] = jnp.transpose(xin[r, i * band : (i + 1) * band, :])
+    for q in range(2 * levels):
+        across(q).wait_recv()
+
+    def ready(level, base):
+        for r in range(2):
+            q = r * levels + level
+            first = flags[r, pl.ds(level, 1), :] < 0.5
+            a, b = vz[0, q], vz[1, q]
+            for h, w in enumerate((jnp.where(first, a, b), jnp.where(first, b, a))):
+                v = split(spread(w[0]))
+                zed = split(jnp.concatenate([w[1], w[2]], axis=1))
+                at = base + r * per_level + h
+                ops[at, 0], ops[at, 1] = zed
+                ops[at, 2], ops[at, 3] = v
+
+    def reflected(base, shift):
+        pairs = [
+            jnp.concatenate([xt[2 * i + shift], xt[2 * i + shift + 1]], axis=1)
+            for i in range(windows)
+        ]
+        halves = [split(pair) for pair in pairs]
+        projected = [
+            split(product(h, (ops[base + i, 0], ops[base + i, 1]), NT))
+            for i, h in enumerate(halves)
+        ]
+        for i, (pair, y) in enumerate(zip(pairs, projected)):
+            new = pair - product(y, (ops[base + i, 2], ops[base + i, 3]))
+            xt[2 * i + shift] = new[:, :band]
+            if 2 * i + shift + 1 < 2 * chunks:
+                xt[2 * i + shift + 1] = new[:, band:]
+
+    ready(0, 0)
+
+    def both_levels(at, carry):
+        ready(2 * at + 1, windows)
+        reflected(0, 0)
+        ready((2 * at + 2) % levels, 0)
+        reflected(windows, 1)
+        return carry
+
+    lax.fori_loop(0, levels // 2, both_levels, 0)
+
+    for i in range(chunks):
+        out_ref[i * band : (i + 1) * band, :] = jnp.transpose(xt[g * chunks + i])
+
+    for zz in range(n_z):
+        q = own + 2 * (zz - z)
+
+        @pl.when(zz != z)
+        def _():
+            to_z(zz).wait_send()
+            relay(q, zz, 0, p1).wait_send()
+            relay(q, zz, 1, p2).wait_send()
+
+        relay(q, zz, 2, p2).wait_send()
+    from_own(n_z, p1).wait_send()
+    from_own(n_z + 1, p2).wait_send()
+    flags_across().wait_send()
+    x_across().wait_send()
+    for q in range(2 * levels):
+        across(q).wait_send()
+
+
+def paired(n_cols, eigvecs, wy_packed, slot_block):
+    band = wy_packed.shape[1]
+    rows, cols = eigvecs.shape
+    levels, per_level = slot_block.shape[1:]
+    n_z = n_cols // 4
+    chunks = rows // band
+    assert n_cols == levels * per_level and 2 * n_z == levels
+    assert wy_packed.shape[0] == 1 and per_level == 2 and chunks == 2 * per_level
+    anywhere = pl.BlockSpec(memory_space=pl.ANY)
+    dma = pltpu.SemaphoreType.DMA
+    return pl.pallas_call(
+        functools.partial(paired_kernel, levels, n_z),
+        out_shape=jax.ShapeDtypeStruct(eigvecs.shape, F32),
+        in_specs=[pl.BlockSpec(memory_space=pltpu.SMEM), anywhere, anywhere],
+        out_specs=pl.BlockSpec(memory_space=pltpu.VMEM),
+        scratch_shapes=[
+            pltpu.VMEM((2 * levels, band, band), F32),
+            pltpu.VMEM((2, 2 * levels, 3, band, band), F32),
+            pltpu.VMEM((2, rows, cols), F32),
+            pltpu.VMEM((2 * chunks + 1, cols, band), F32),
+            pltpu.VMEM((4 * per_level, 4, band, 2 * band), BF16),
+            pltpu.VMEM((2, levels, band), F32),
+            dma((2 * levels,)),
+            dma((n_z + 2,)),
+            dma((n_z, 3)),
+            dma((2 * levels,)),
+            dma((2 * levels,)),
+            dma((2, 2)),
+            dma((2,)),
+        ],
+        compiler_params=pltpu.CompilerParams(collective_id=0, has_side_effects=True),
+    )(jnp.swapaxes(slot_block, 1, 2), eigvecs, wy_packed)
+
+
 def kernel(
     levels, n_rows, n_z, slot_ref, eig_ref, wy_ref, out_ref,
     wg, xt, ops, half_send, above, up_send, up_recv, down_send, down_recv,
@@ -198,14 +427,6 @@
     for i in range(chunks):
         xt[i] = jnp.transpose(eig_ref[i * band : (i + 1) * band, :])
 
-    row = lax.broadcasted_iota(jnp.int32, (band, band), 0)
-    col = lax.broadcasted_iota(jnp.int32, (band, band), 1)
-    upper = col >= row
-    zero = jnp.zeros((band, band), F32)
-
-    def spread(w):
-        return jnp.concatenate([jnp.where(upper, w, zero), jnp.where(upper, zero, w)], axis=1)
-
     def chosen(level, h):
         first = slot_ref[0, h, level] == 0
         return jnp.where(first, wg[level * per_level], wg[level * per_level + 1])
@@ -344,6 +565,8 @@
 
 
 def per_device(n_rows, n_cols, eigvecs, wy_packed, slot_block):
+    if n_rows == 2:
+        return paired(n_cols, eigvecs, wy_packed, slot_block)
     band = wy_packed.shape[1]
     rows, cols = eigvecs.shape
     levels, per_level = slot_block.shape[1:]

time: 38.3 us -> 38.2 us (level)
  the two profiles are of different devices: /device:TPU:8 before, /device:TPU:1 now
where the time goes in v1:
time: 38.2 us; the launch traced here: 38.1 us
  Pallas kernels  36.4 us (95%)
  local copies, waits for them, and re-layouts  1.67 us (4%)
    pallas_call x1, Pallas kernels, paired(): pl.pallas_call(functools.partial(paired_kernel, levels, n_z), out_shape=j...  36.4 us
    unnamed x1, local copies, waits for them, and re-layouts  1.67 us

profile of v1, /device:TPU:1, one launch (start us, length us, event | category | flops | bytes accessed | tf_op | source)
XLA Modules:
  0.0 38.1 jit_solution(256969717486453606)
XLA Ops:
  0.0 36.4 %shard_map.37 = f32[512,128]{1,0:T(8,128)} custom-call(s32[1,2,8]{2,1,0:T(2,128)} %bitcast.1, f32[512,128]{1,0:T(8,128)} %eig_ref.1, f32[1,128,128]{2,1,0:T(8,128)} %wy_ref.1), custom_call_target="tpu_custom_call" | custom-call | tf_op jit(solution)/shard_map/pallas_call | solution.py:272
  36.4 1.7 %copy.5 = f32[512,128]{1,0:T(8,128)} copy(f32[512,128]{1,0:T(8,128)} %shard_map.37) | data formatting | bytes 524288

commit v2 on v1

--- a/solution.py
+++ b/solution.py
@@ -30,22 +30,47 @@
 
 def inverses(grams, multiply):
     band = grams[0].shape[0]
+    small = 16
     row = lax.broadcasted_iota(jnp.int32, (band, band), 0)
     col = lax.broadcasted_iota(jnp.int32, (band, band), 1)
     zero = jnp.zeros((band, band), F32)
-    diagonal = row == col
-    stricts, found = [], []
-    for gram in grams:
-        on_diagonal = jnp.where(diagonal, 0.5 * gram, zero)
-        by_row = 1.0 / jnp.sum(on_diagonal, axis=1, keepdims=True)
-        by_col = 1.0 / jnp.sum(on_diagonal, axis=0, keepdims=True)
-        strict = jnp.where(col > row, gram, zero)
-        pairs = jnp.where(row // 2 == col // 2, strict, zero)
-        stricts.append(strict)
-        found.append(jnp.where(diagonal, by_row, zero) - pairs * by_row * by_col)
-    width = 2
+    upper = col > row
+    near = row // small == col // small
+    stricts = [jnp.where(upper, gram, zero) for gram in grams]
+
+    at = lax.broadcasted_iota(jnp.int32, (small, band), 0)
+    lane = lax.broadcasted_iota(jnp.int32, (small, band), 1)
+    first = lane // small * small
+    on_diagonal = lane - first == at
+    none = jnp.zeros((small, band), F32)
+
+    def gathered(value, index):
+        return jnp.take_along_axis(value, index, axis=1)
+
+    def side_by_side(value):
+        parts = [value[i : i + small] for i in range(0, band, small)]
+        return functools.reduce(jnp.add, parts)
+
+    packed = [side_by_side(jnp.where(near, gram, zero)) for gram in grams]
+    scales = [
+        2.0 / jnp.sum(jnp.where(on_diagonal, p, none), axis=0, keepdims=True) for p in packed
+    ]
+    scaled = [
+        jnp.where(lane - first > at, p, none) * s for p, s in zip(packed, scales)
+    ]
+    solved = [jnp.where(on_diagonal, 1.0, none) for _ in grams]
+    for m in range(small - 1, 0, -1):
+        columns = [gathered(s, first + m) for s in scaled]
+        solved = [r - a * r[m : m + 1] for r, a in zip(solved, columns)]
+    by_row = [gathered(jnp.broadcast_to(s, (small, band)), first + at) for s in scales]
+    solved = [r * s for r, s in zip(solved, by_row)]
+    found = [
+        jnp.where(near, jnp.concatenate([r] * (band // small), axis=0), zero) for r in solved
+    ]
+
+    width = small
     while width < band:
-        factor = 4 if width * 4 <= band else 2
+        factor = 2 if band // width % 4 else 4
         wide = width * factor
         inside = (row // wide == col // wide) & (row // width != col // width)
         corners = [jnp.where(inside, strict, zero) for strict in stricts]
@@ -93,8 +118,8 @@
     c = lax.axis_index("cols")
     z, x, k = c // 4, (c // 2) % 2, c % 2
     flip_g, flip_x = 1 - 2 * g, 1 - 2 * x
-    p1 = {"rows": g + (1 - k) * flip_g, "cols": c + k * 2 * flip_x}
-    p2 = {"rows": g + k * flip_g, "cols": c + (1 - k) * 2 * flip_x}
+    p1 = {"rows": 1 - g, "cols": c}
+    p2 = {"rows": g, "cols": c + 2 * flip_x}
     core_partner = {"rows": g, "cols": c + 1 - 2 * k}
     row_partner = {"rows": 1 - g, "cols": c}
 
@@ -155,13 +180,12 @@
     from_own(n_z, p1).start()
     from_own(n_z + 1, p2).start()
     flags_across().start()
-    x_across().start()
     local_v.wait()
 
     def line(j, carry):
         f1, f2 = j % 2, j // 2
-        line_g = g + flip_g * (k * f2 + (1 - k) * f1)
-        line_x = x + flip_x * (k * f1 + (1 - k) * f2)
+        line_g = g + flip_g * f1
+        line_x = x + flip_x * f2
         blocks = [line_g * levels + zz * 2 + line_x for zz in range(n_z)]
         for zz in range(n_z - 1, -1, -1):
             q = blocks[zz]
@@ -178,6 +202,10 @@
             @pl.when(j == 1)
             def _():
                 relay(q, zz, 2, p2).start()
+
+        @pl.when(j == 0)
+        def _():
+            x_across().start()
 
         sheared = [pltpu.roll(jnp.transpose(raw[q]), 0, 1, stride=1, stride_axis=0) for q in blocks]
         for q, w, zed in zip(blocks, sheared, own_blocks(sheared)):

time: 38.2 us -> 35.2 us (0.921)
  Pallas kernels: 36.4 us -> 33.3 us
    pallas_call x1, Pallas kernels: 36.4 us -> 33.3 us  [paired(): pl.pallas_call(functools.partial(paired_kernel, levels, n_z), out_shape=j...]
where the time goes in v2:
time: 35.2 us; the launch traced here: 35 us
  Pallas kernels  33.3 us (95%)
  local copies, waits for them, and re-layouts  1.67 us (5%)
    pallas_call x1, Pallas kernels, paired(): pl.pallas_call(functools.partial(paired_kernel, levels, n_z), out_shape=j...  33.3 us
    unnamed x1, local copies, waits for them, and re-layouts  1.67 us

profile of v2, /device:TPU:1, one launch (start us, length us, event | category | flops | bytes accessed | tf_op | source)
XLA Modules:
  0.0 35.0 jit_solution(2875021916746889801)
XLA Ops:
  0.0 33.3 %shard_map.37 = f32[512,128]{1,0:T(8,128)} custom-call(s32[1,2,8]{2,1,0:T(2,128)} %bitcast.1, f32[512,128]{1,0:T(8,128)} %eig_ref.1, f32[1,128,128]{2,1,0:T(8,128)} %wy_ref.1), custom_call_target="tpu_custom_call" | custom-call | tf_op jit(solution)/shard_map/pallas_call | solution.py:300
  33.4 1.7 %copy.5 = f32[512,128]{1,0:T(8,128)} copy(f32[512,128]{1,0:T(8,128)} %shard_map.37) | data formatting | bytes 524288

commit v3 on v2

--- a/solution.py
+++ b/solution.py
@@ -120,6 +120,7 @@
     flip_g, flip_x = 1 - 2 * g, 1 - 2 * x
     p1 = {"rows": 1 - g, "cols": c}
     p2 = {"rows": g, "cols": c + 2 * flip_x}
+    p3 = {"rows": 1 - g, "cols": c + 2 * flip_x}
     core_partner = {"rows": g, "cols": c + 1 - 2 * k}
     row_partner = {"rows": 1 - g, "cols": c}
 
@@ -127,6 +128,7 @@
         return {"rows": g, "cols": c + 4 * (zz - z)}
 
     own = g * levels + z * 2 + x
+    opposite = (1 - g) * levels + z * 2 + 1 - x
 
     local_v = pltpu.make_async_copy(wy_ref.at[0], raw.at[own], local_sem.at[0])
     local_x = pltpu.make_async_copy(eig_ref, xin.at[g], local_sem.at[1])
@@ -138,7 +140,7 @@
         pl.semaphore_signal(
             barrier, inc=1, device_id=z_mate((z + d) % n_z), device_id_type=MESH
         )
-    for other in (p1, p2, core_partner):
+    for other in (p1, p2, p3, core_partner):
         pl.semaphore_signal(barrier, inc=1, device_id=other, device_id_type=MESH)
 
     level_row = lax.broadcasted_iota(jnp.int32, (levels, band), 0)
@@ -155,7 +157,7 @@
         )
 
     def from_own(at, target):
-        return remote(wy_ref.at[0], raw.at[own], own_send.at[at], raw_recv.at[own], target)
+        return remote(raw.at[own], raw.at[own], own_send.at[at], raw_recv.at[own], target)
 
     def to_z(zz):
         return from_own(zz, z_mate(zz))
@@ -172,7 +174,13 @@
     def x_across():
         return remote(eig_ref, xin.at[g], side_sem.at[0, 1], side_sem.at[1, 1], row_partner)
 
-    pl.semaphore_wait(barrier, n_z + 2)
+    local_v.wait()
+    pl.semaphore_wait(barrier, n_z + 3)
+
+    @pl.when(k == 0)
+    def _():
+        from_own(n_z + 2, p3).start()
+
     for zz in range(n_z - 1, -1, -1):
         @pl.when(zz != z)
         def _():
@@ -180,33 +188,49 @@
     from_own(n_z, p1).start()
     from_own(n_z + 1, p2).start()
     flags_across().start()
-    local_v.wait()
-
-    def line(j, carry):
-        f1, f2 = j % 2, j // 2
-        line_g = g + flip_g * f1
-        line_x = x + flip_x * f2
-        blocks = [line_g * levels + zz * 2 + line_x for zz in range(n_z)]
-        for zz in range(n_z - 1, -1, -1):
-            q = blocks[zz]
-
-            @pl.when((j > 0) | (zz != z))
-            def _():
-                relay(q, zz, 0, p1).wait_recv()
-
-            @pl.when((j == 0) & (zz != z))
-            def _():
-                relay(q, zz, 0, p1).start()
-                relay(q, zz, 1, p2).start()
-
-            @pl.when(j == 1)
-            def _():
-                relay(q, zz, 2, p2).start()
-
-        @pl.when(j == 0)
-        def _():
+
+    side = jnp.where(z < n_z // 2, 1, n_z - 1)
+
+    def plane(step, carry):
+        zz = (z + side * step) % n_z
+        at = zz * 2 + x
+        mine = g * levels + at
+        across_y = (1 - g) * levels + at
+        across_x = g * levels + at + flip_x
+        across_both = (1 - g) * levels + at + flip_x
+        blocks = [mine, across_y, across_x, across_both]
+
+        @pl.when((step == 0) & (k == 0))
+        def _():
+            relay(across_both, 0, 0, p1).wait_recv()
+            for d in range(n_z - 1, 0, -1):
+                far = (z + d) % n_z
+                relay(opposite, far, 2, z_mate(far)).start()
+
+        @pl.when((step == 0) & (k == 1))
+        def _():
+            relay(across_y, 0, 0, p1).wait_recv()
+            relay(across_y, z, 2, p2).start()
+
+        @pl.when(step == 0)
+        def _():
+            for d in range(1, n_z):
+                far = (z + side * d) % n_z
+                q = g * levels + far * 2 + x
+                relay(q, far, 0, p1).wait_recv()
+                relay(q, far, 0, p1).start()
+                relay(q, far, 1, p2).start()
             x_across().start()
 
+        @pl.when(k == 0)
+        def _():
+            relay(across_y, 0, 0, p1).wait_recv()
+
+        @pl.when((step > 0) | (k == 1))
+        def _():
+            relay(across_both, 0, 0, p1).wait_recv()
+
+        relay(across_x, 0, 0, p1).wait_recv()
         sheared = [pltpu.roll(jnp.transpose(raw[q]), 0, 1, stride=1, stride_axis=0) for q in blocks]
         for q, w, zed in zip(blocks, sheared, own_blocks(sheared)):
             vz[k, q, 0] = w
@@ -214,9 +238,18 @@
             vz[k, q, 2] = zed[:, band:]
         for q in blocks:
             across(q).start()
+
+        @pl.when((step == 0) & (k == 1))
+        def _():
+            for d in range(1, n_z):
+                far = (z + side * d) % n_z
+                q = (1 - g) * levels + far * 2 + x
+                relay(q, far, 0, p1).wait_recv()
+                relay(q, far, 2, p2).start()
+
         return carry
 
-    lax.fori_loop(0, 4, line, 0)
+    lax.fori_loop(0, n_z, plane, 0)
 
     local_x.wait()
     x_across().wait_recv()
@@ -278,9 +311,17 @@
             relay(q, zz, 0, p1).wait_send()
             relay(q, zz, 1, p2).wait_send()
 
-        relay(q, zz, 2, p2).wait_send()
+        @pl.when((zz != z) | (k == 1))
+        def _():
+            relay(q, zz, 2, p2).wait_send()
+
     from_own(n_z, p1).wait_send()
     from_own(n_z + 1, p2).wait_send()
+
+    @pl.when(k == 0)
+    def _():
+        from_own(n_z + 2, p3).wait_send()
+
     flags_across().wait_send()
     x_across().wait_send()
     for q in range(2 * levels):
@@ -310,7 +351,7 @@
             pltpu.VMEM((4 * per_level, 4, band, 2 * band), BF16),
             pltpu.VMEM((2, levels, band), F32),
             dma((2 * levels,)),
-            dma((n_z + 2,)),
+            dma((n_z + 3,)),
             dma((n_z, 3)),
             dma((2 * levels,)),
             dma((2 * levels,)),

time: 35.2 us -> 32.1 us (0.912)
  the two profiles are of different devices: /device:TPU:1 before, /device:TPU:0 now
where the time goes in v3:
time: 32.1 us; the launch traced here: 31.8 us
  Pallas kernels  30.1 us (94%)
  local copies, waits for them, and re-layouts  1.67 us (5%)
    pallas_call x1, Pallas kernels, paired(): pl.pallas_call(functools.partial(paired_kernel, levels, n_z), out_shape=j...  30.1 us
    unnamed x1, local copies, waits for them, and re-layouts  1.67 us

profile of v3, /device:TPU:0, one launch (start us, length us, event | category | flops | bytes accessed | tf_op | source)
XLA Modules:
  0.0 31.8 jit_solution(13087882756065490126)
XLA Ops:
  0.0 30.1 %shard_map.37 = f32[512,128]{1,0:T(8,128)} custom-call(s32[1,2,8]{2,1,0:T(2,128)} %bitcast.1, f32[512,128]{1,0:T(8,128)} %eig_ref.1, f32[1,128,128]{2,1,0:T(8,128)} %wy_ref.1), custom_call_target="tpu_custom_call" | custom-call | tf_op jit(solution)/shard_map/pallas_call | solution.py:341
  30.1 1.7 %copy.5 = f32[512,128]{1,0:T(8,128)} copy(f32[512,128]{1,0:T(8,128)} %shard_map.37) | data formatting | bytes 524288

commit v4 on v3

--- a/solution.py
+++ b/solution.py
@@ -189,10 +189,11 @@
     from_own(n_z + 1, p2).start()
     flags_across().start()
 
-    side = jnp.where(z < n_z // 2, 1, n_z - 1)
-
-    def plane(step, carry):
-        zz = (z + side * step) % n_z
+    def other(i):
+        return i + (z <= i).astype(jnp.int32)
+
+    def plane(step):
+        zz = jnp.where(step == 0, z, other(step - 1))
         at = zz * 2 + x
         mine = g * levels + at
         across_y = (1 - g) * levels + at
@@ -214,8 +215,8 @@
 
         @pl.when(step == 0)
         def _():
-            for d in range(1, n_z):
-                far = (z + side * d) % n_z
+            for i in range(n_z - 1):
+                far = other(i)
                 q = g * levels + far * 2 + x
                 relay(q, far, 0, p1).wait_recv()
                 relay(q, far, 0, p1).start()
@@ -241,24 +242,12 @@
 
         @pl.when((step == 0) & (k == 1))
         def _():
-            for d in range(1, n_z):
-                far = (z + side * d) % n_z
+            for i in range(n_z - 1):
+                far = other(i)
                 q = (1 - g) * levels + far * 2 + x
                 relay(q, far, 0, p1).wait_recv()
                 relay(q, far, 2, p2).start()
 
-        return carry
-
-    lax.fori_loop(0, n_z, plane, 0)
-
-    local_x.wait()
-    x_across().wait_recv()
-    flags_across().wait_recv()
-    for r in range(2):
-        for i in range(chunks):
-            xt[r * chunks + i] = jnp.transpose(xin[r, i * band : (i + 1) * band, :])
-    for q in range(2 * levels):
-        across(q).wait_recv()
 
     def ready(level, base):
         for r in range(2):
@@ -288,16 +277,36 @@
             if 2 * i + shift + 1 < 2 * chunks:
                 xt[2 * i + shift + 1] = new[:, band:]
 
-    ready(0, 0)
-
-    def both_levels(at, carry):
+    def both_levels(at):
+        @pl.when(at == 0)
+        def _():
+            local_x.wait()
+            x_across().wait_recv()
+            flags_across().wait_recv()
+            for r in range(2):
+                for i in range(chunks):
+                    xt[r * chunks + i] = jnp.transpose(xin[r, i * band : (i + 1) * band, :])
+
+        for i in range(2):
+            for r in range(2):
+                across(r * levels + 2 * at + i).wait_recv()
+        ready(2 * at, 0)
         ready(2 * at + 1, windows)
         reflected(0, 0)
-        ready((2 * at + 2) % levels, 0)
         reflected(windows, 1)
+
+    def turn(step, carry):
+        @pl.when(step < n_z)
+        def _():
+            plane(step)
+
+        @pl.when(step >= 2)
+        def _():
+            both_levels(step - 2)
+
         return carry
 
-    lax.fori_loop(0, levels // 2, both_levels, 0)
+    lax.fori_loop(0, n_z + 2, turn, 0)
 
     for i in range(chunks):
         out_ref[i * band : (i + 1) * band, :] = jnp.transpose(xt[g * chunks + i])

time: 32.1 us -> 30.8 us (0.960)
  Pallas kernels: 30.1 us -> 28.9 us
    pallas_call x1, Pallas kernels: 30.1 us -> 28.9 us  [paired(): pl.pallas_call(functools.partial(paired_kernel, levels, n_z), out_shape=j...]
where the time goes in v4:
time: 30.8 us; the launch traced here: 30.5 us
  Pallas kernels  28.9 us (94%)
  local copies, waits for them, and re-layouts  1.67 us (5%)
    pallas_call x1, Pallas kernels, paired(): pl.pallas_call(functools.partial(paired_kernel, levels, n_z), out_shape=j...  28.9 us
    unnamed x1, local copies, waits for them, and re-layouts  1.67 us

profile of v4, /device:TPU:0, one launch (start us, length us, event | category | flops | bytes accessed | tf_op | source)
XLA Modules:
  0.0 30.5 jit_solution(74443518246011685)
XLA Ops:
  0.0 28.9 %shard_map.37 = f32[512,128]{1,0:T(8,128)} custom-call(s32[1,2,8]{2,1,0:T(2,128)} %bitcast.1, f32[512,128]{1,0:T(8,128)} %eig_ref.1, f32[1,128,128]{2,1,0:T(8,128)} %wy_ref.1), custom_call_target="tpu_custom_call" | custom-call | tf_op jit(solution)/shard_map/pallas_call | solution.py:350
  28.9 1.7 %copy.5 = f32[512,128]{1,0:T(8,128)} copy(f32[512,128]{1,0:T(8,128)} %shard_map.37) | data formatting | bytes 524288

commit v5 on v4

--- a/solution.py
+++ b/solution.py
@@ -124,6 +124,14 @@
     core_partner = {"rows": g, "cols": c + 1 - 2 * k}
     row_partner = {"rows": 1 - g, "cols": c}
 
+    side = jnp.where(z < n_z // 2, 1, n_z - 1)
+
+    def near(i):
+        return (z + side * (i + 1)) % n_z
+
+    def upward(i):
+        return i + (z <= i).astype(jnp.int32)
+
     def z_mate(zz):
         return {"rows": g, "cols": c + 4 * (zz - z)}
 
@@ -181,19 +189,14 @@
     def _():
         from_own(n_z + 2, p3).start()
 
-    for zz in range(n_z - 1, -1, -1):
-        @pl.when(zz != z)
-        def _():
-            to_z(zz).start()
+    for i in range(n_z - 1):
+        to_z(near(i)).start()
     from_own(n_z, p1).start()
     from_own(n_z + 1, p2).start()
     flags_across().start()
 
-    def other(i):
-        return i + (z <= i).astype(jnp.int32)
-
     def plane(step):
-        zz = jnp.where(step == 0, z, other(step - 1))
+        zz = jnp.where(step == 0, z, upward(step - 1))
         at = zz * 2 + x
         mine = g * levels + at
         across_y = (1 - g) * levels + at
@@ -216,7 +219,7 @@
         @pl.when(step == 0)
         def _():
             for i in range(n_z - 1):
-                far = other(i)
+                far = upward(i)
                 q = g * levels + far * 2 + x
                 relay(q, far, 0, p1).wait_recv()
                 relay(q, far, 0, p1).start()
@@ -243,7 +246,7 @@
         @pl.when((step == 0) & (k == 1))
         def _():
             for i in range(n_z - 1):
-                far = other(i)
+                far = upward(i)
                 q = (1 - g) * levels + far * 2 + x
                 relay(q, far, 0, p1).wait_recv()
                 relay(q, far, 2, p2).start()
@@ -300,13 +303,13 @@
         def _():
             plane(step)
 
-        @pl.when(step >= 2)
-        def _():
-            both_levels(step - 2)
+        @pl.when(step >= 3)
+        def _():
+            both_levels(step - 3)
 
         return carry
 
-    lax.fori_loop(0, n_z + 2, turn, 0)
+    lax.fori_loop(0, n_z + 3, turn, 0)
 
     for i in range(chunks):
         out_ref[i * band : (i + 1) * band, :] = jnp.transpose(xt[g * chunks + i])

time: 30.8 us -> 29.7 us (0.964)
  Pallas kernels: 28.9 us -> 27.6 us
    pallas_call x1, Pallas kernels: 28.9 us -> 27.6 us  [paired(): pl.pallas_call(functools.partial(paired_kernel, levels, n_z), out_shape=j...]
where the time goes in v5:
time: 29.7 us; the launch traced here: 29.3 us
  Pallas kernels  27.6 us (93%)
  local copies, waits for them, and re-layouts  1.67 us (6%)
    pallas_call x1, Pallas kernels, paired(): pl.pallas_call(functools.partial(paired_kernel, levels, n_z), out_shape=j...  27.6 us
    unnamed x1, local copies, waits for them, and re-layouts  1.67 us

profile of v5, /device:TPU:0, one launch (start us, length us, event | category | flops | bytes accessed | tf_op | source)
XLA Modules:
  0.0 29.3 jit_solution(10561670144125098201)
XLA Ops:
  0.0 27.6 %shard_map.37 = f32[512,128]{1,0:T(8,128)} custom-call(s32[1,2,8]{2,1,0:T(2,128)} %bitcast.1, f32[512,128]{1,0:T(8,128)} %eig_ref.1, f32[1,128,128]{2,1,0:T(8,128)} %wy_ref.1), custom_call_target="tpu_custom_call" | custom-call | tf_op jit(solution)/shard_map/pallas_call | solution.py:353
  27.6 1.7 %copy.5 = f32[512,128]{1,0:T(8,128)} copy(f32[512,128]{1,0:T(8,128)} %shard_map.37) | data formatting | bytes 524288

commit v6 on v5

--- a/solution.py
+++ b/solution.py
@@ -24,8 +24,16 @@
     dot = functools.partial(lax.dot_general, dimension_numbers=dims, preferred_element_type=F32)
     if dims == NN:
         stacked = jnp.concatenate([a[0], a[1]], axis=1)
+        cols = b[0].shape[1]
+        if cols == a[0].shape[1]:
+            upper = jnp.concatenate([b[0], b[1]], axis=1)
+            lower = jnp.concatenate([b[0], jnp.zeros_like(b[1])], axis=1)
+            both = dot(stacked, jnp.concatenate([upper, lower], axis=0))
+            return both[:, :cols] + both[:, cols:]
         return dot(stacked, jnp.concatenate([b[0], b[0]], axis=0)) + dot(a[0], b[1])
-    return dot(a[0], b[0]) + (dot(a[0], b[1]) + dot(a[1], b[0]))
+    both = dot(a[0], jnp.concatenate([b[0], b[1]], axis=0))
+    rows = b[0].shape[0]
+    return both[:, :rows] + (both[:, rows:] + dot(a[1], b[0]))
 
 
 def inverses(grams, multiply):

time: 29.7 us -> 28.7 us (0.966)
  Pallas kernels: 27.6 us -> 26.7 us
    pallas_call x1, Pallas kernels: 27.6 us -> 26.7 us  [paired(): pl.pallas_call(functools.partial(paired_kernel, levels, n_z), out_shape=j...]
where the time goes in v6:
time: 28.7 us; the launch traced here: 28.4 us
  Pallas kernels  26.7 us (93%)
  local copies, waits for them, and re-layouts  1.67 us (6%)
    pallas_call x1, Pallas kernels, paired(): pl.pallas_call(functools.partial(paired_kernel, levels, n_z), out_shape=j...  26.7 us
    unnamed x1, local copies, waits for them, and re-layouts  1.67 us

profile of v6, /device:TPU:0, one launch (start us, length us, event | category | flops | bytes accessed | tf_op | source)
XLA Modules:
  0.0 28.4 jit_solution(11563792951325700640)
XLA Ops:
  0.0 26.7 %shard_map.37 = f32[512,128]{1,0:T(8,128)} custom-call(s32[1,2,8]{2,1,0:T(2,128)} %bitcast.1, f32[512,128]{1,0:T(8,128)} %eig_ref.1, f32[1,128,128]{2,1,0:T(8,128)} %wy_ref.1), custom_call_target="tpu_custom_call" | custom-call | tf_op jit(solution)/shard_map/pallas_call | solution.py:361
  26.7 1.7 %copy.5 = f32[512,128]{1,0:T(8,128)} copy(f32[512,128]{1,0:T(8,128)} %shard_map.37) | data formatting | bytes 524288

commit v7 on v6

--- a/solution.py
+++ b/solution.py
@@ -203,6 +203,15 @@
     from_own(n_z + 1, p2).start()
     flags_across().start()
 
+    def factor(blocks):
+        sheared = [pltpu.roll(jnp.transpose(raw[q]), 0, 1, stride=1, stride_axis=0) for q in blocks]
+        for q, w, zed in zip(blocks, sheared, own_blocks(sheared)):
+            vz[k, q, 0] = w
+            vz[k, q, 1] = zed[:, :band]
+            vz[k, q, 2] = zed[:, band:]
+        for q in blocks:
+            across(q).start()
+
     def plane(step):
         zz = jnp.where(step == 0, z, upward(step - 1))
         at = zz * 2 + x
@@ -243,13 +252,6 @@
             relay(across_both, 0, 0, p1).wait_recv()
 
         relay(across_x, 0, 0, p1).wait_recv()
-        sheared = [pltpu.roll(jnp.transpose(raw[q]), 0, 1, stride=1, stride_axis=0) for q in blocks]
-        for q, w, zed in zip(blocks, sheared, own_blocks(sheared)):
-            vz[k, q, 0] = w
-            vz[k, q, 1] = zed[:, :band]
-            vz[k, q, 2] = zed[:, band:]
-        for q in blocks:
-            across(q).start()
 
         @pl.when((step == 0) & (k == 1))
         def _():
@@ -258,6 +260,8 @@
                 q = (1 - g) * levels + far * 2 + x
                 relay(q, far, 0, p1).wait_recv()
                 relay(q, far, 2, p2).start()
+
+        return blocks
 
 
     def ready(level, base):
@@ -307,17 +311,21 @@
         reflected(windows, 1)
 
     def turn(step, carry):
-        @pl.when(step < n_z)
-        def _():
-            plane(step)
-
-        @pl.when(step >= 3)
-        def _():
-            both_levels(step - 3)
+        @pl.when(step < n_z - 2)
+        def _():
+            factor(plane(step))
+
+        @pl.when(step == n_z - 2)
+        def _():
+            factor(plane(n_z - 2) + plane(n_z - 1))
+
+        @pl.when(step >= n_z - 2)
+        def _():
+            both_levels(step - (n_z - 2))
 
         return carry
 
-    lax.fori_loop(0, n_z + 3, turn, 0)
+    lax.fori_loop(0, 2 * n_z - 2, turn, 0)
 
     for i in range(chunks):
         out_ref[i * band : (i + 1) * band, :] = jnp.transpose(xt[g * chunks + i])

time: 28.7 us -> 28.3 us (0.986)
  no operation moved by 1% of the time
where the time goes in v7:
time: 28.3 us; the launch traced here: 28.2 us
  Pallas kernels  26.5 us (94%)
  local copies, waits for them, and re-layouts  1.67 us (6%)
    pallas_call x1, Pallas kernels, paired(): pl.pallas_call(functools.partial(paired_kernel, levels, n_z), out_shape=j...  26.5 us
    unnamed x1, local copies, waits for them, and re-layouts  1.67 us

profile of v7, /device:TPU:0, one launch (start us, length us, event | category | flops | bytes accessed | tf_op | source)
XLA Modules:
  0.0 28.2 jit_solution(11657475346514635024)
XLA Ops:
  0.0 26.5 %shard_map.37 = f32[512,128]{1,0:T(8,128)} custom-call(s32[1,2,8]{2,1,0:T(2,128)} %bitcast.1, f32[512,128]{1,0:T(8,128)} %eig_ref.1, f32[1,128,128]{2,1,0:T(8,128)} %wy_ref.1), custom_call_target="tpu_custom_call" | custom-call | tf_op jit(solution)/shard_map/pallas_call | solution.py:369
  26.5 1.7 %copy.5 = f32[512,128]{1,0:T(8,128)} copy(f32[512,128]{1,0:T(8,128)} %shard_map.37) | data formatting | bytes 524288

commit v8 on v7

--- a/solution.py
+++ b/solution.py
@@ -311,21 +311,17 @@
         reflected(windows, 1)
 
     def turn(step, carry):
-        @pl.when(step < n_z - 2)
-        def _():
-            factor(plane(step))
-
-        @pl.when(step == n_z - 2)
-        def _():
-            factor(plane(n_z - 2) + plane(n_z - 1))
-
-        @pl.when(step >= n_z - 2)
-        def _():
-            both_levels(step - (n_z - 2))
+        @pl.when(step < n_z // 2)
+        def _():
+            factor(plane(2 * step) + plane(2 * step + 1))
+
+        @pl.when(step >= n_z // 2 - 1)
+        def _():
+            both_levels(step - (n_z // 2 - 1))
 
         return carry
 
-    lax.fori_loop(0, 2 * n_z - 2, turn, 0)
+    lax.fori_loop(0, n_z + n_z // 2 - 1, turn, 0)
 
     for i in range(chunks):
         out_ref[i * band : (i + 1) * band, :] = jnp.transpose(xt[g * chunks + i])

time: 28.3 us -> 28.3 us (level)
  no operation moved by 1% of the time
where the time goes in v8:
time: 28.3 us; the launch traced here: 28.1 us
  Pallas kernels  26.5 us (94%)
  local copies, waits for them, and re-layouts  1.67 us (6%)
    pallas_call x1, Pallas kernels, paired(): pl.pallas_call(functools.partial(paired_kernel, levels, n_z), out_shape=j...  26.5 us
    unnamed x1, local copies, waits for them, and re-layouts  1.67 us

profile of v8, /device:TPU:0, one launch (start us, length us, event | category | flops | bytes accessed | tf_op | source)
XLA Modules:
  0.0 28.1 jit_solution(1477699036583995861)
XLA Ops:
  0.0 26.5 %shard_map.37 = f32[512,128]{1,0:T(8,128)} custom-call(s32[1,2,8]{2,1,0:T(2,128)} %bitcast.1, f32[512,128]{1,0:T(8,128)} %eig_ref.1, f32[1,128,128]{2,1,0:T(8,128)} %wy_ref.1), custom_call_target="tpu_custom_call" | custom-call | tf_op jit(solution)/shard_map/pallas_call | solution.py:365
  26.5 1.7 %copy.5 = f32[512,128]{1,0:T(8,128)} copy(f32[512,128]{1,0:T(8,128)} %shard_map.37) | data formatting | bytes 524288
